TPU v7x, 128 devices: a whole 4x4x4 slice. The times are simulated.
128 devices in a mesh: seq: 8 (over z, core), head: 16 (over x, y).
Axes of the slice: x: 4, y: 4, z: 4, core: 2. Of those that a mesh axis runs over, the one named last changes fastest.
Arguments:
- query_raw: bfloat16 [8192, 8192], P('seq', 'head'), may hold values from -12 to 12
- key_raw: bfloat16 [8192, 8192], P('seq', 'head'), may hold values from -6 to 6
- value_raw: bfloat16 [8192, 8192], P('seq', 'head'), may hold values from -6 to 6
- query_gain: float32 [8192], P('head'), may hold values from 0.1 to 1.9
- log_decay: float32 [64, 8192], P('head', 'seq'), may hold values from -1.5 to 0
- out_grad: bfloat16 [8192, 8192], P('seq', 'head'), may hold values from -0.75 to 0.75
Outputs:
- query_raw_grad: bfloat16 [8192, 8192], P(('seq', 'head'))
- key_raw_grad: bfloat16 [8192, 8192], P(('seq', 'head'))
- value_raw_grad: bfloat16 [8192, 8192], P(('seq', 'head'))
All inputs are finite; a program needn't handle non-finite values.
Results may differ from a plain program's by a relative error of at most 0.0021.
Values may be sent and summed in bfloat16 or wider, within the bound.
No kernel may reach another device: no remote copies, remote signals or barrier semaphores. Data moves between devices by JAX's collectives and lax.ppermute only.
A program may use at most 128 MiB of HBM per device.

v0:
```python
import functools
import jax
import jax.numpy as jnp
from jax import lax
from jax.sharding import Mesh
from jax.sharding import PartitionSpec as P

D = 8192
BLOCK = 128
HEAD = ("head_0", "head_1")
SEQ = ("seq_0", "seq_1")
SEQ_HEAD = ("seq_0", "seq_1", "head_0", "head_1")
epsilon = 1e-06


def from_everyone(value, axis):
    length = lax.axis_size(axis)
    return lax.all_to_all(
        jnp.broadcast_to(value[None], (length, *value.shape)), axis, 0, 0, tiled=True
    )


def taken_together(value, axis):
    return from_everyone(value, axis).sum(axis=0)


def carried_in(value, axis, combine, identity):
    length, mine = (lax.axis_size(axis), lax.axis_index(axis))
    everything = jax.tree.map(lambda part: lax.all_gather(part, axis), value)
    start = jax.tree.map(
        lambda part, zero: jnp.broadcast_to(jnp.asarray(zero, part.dtype), part.shape),
        value,
        identity,
    )

    def lap(k, before):
        reached = k < mine
        new = combine(before, jax.tree.map(lambda part: part[k], everything))
        return jax.tree.map(lambda a, b: jnp.where(reached, a, b), new, before)

    return lax.fori_loop(0, length, lap, start)


def nothing_yet(value, identity):
    return jax.tree.map(
        lambda part, zero: jnp.zeros_like(part) + jnp.asarray(zero, part.dtype), value, identity
    )


def carried_in_2(value, axes, combine, identity):
    before = start = nothing_yet(value, identity)
    subtotal = value
    for axis in reversed(axes):
        length, mine = (lax.axis_size(axis), lax.axis_index(axis))
        pieces = jax.tree.map(lambda part: lax.all_gather(part, axis), subtotal)
        inside, subtotal = (start, start)
        for k in reversed(range(length)):
            passed = k > mine
            subtotal = combine(subtotal, jax.tree.map(lambda part: part[k], pieces))
            inside = jax.tree.map(lambda new, old: jnp.where(passed, new, old), subtotal, inside)
        before = combine(inside, before)
    return before


def by_axis(value, axes):
    return functools.reduce(lax.psum, axes, value)


def exact_prod(form, left, right):
    return jnp.einsum(form, left, right, precision=lax.Precision.HIGHEST)


def block_parts(queries, keys, gates):
    size = gates.shape[0]
    cumul = jnp.cumsum(gates)
    element_slot = lax.broadcasted_iota(jnp.int32, (size, size), 0)
    column = lax.broadcasted_iota(jnp.int32, (size, size), 1)
    causal = element_slot >= column
    strict = element_slot > column
    spread = jnp.where(causal, cumul[:, None] - cumul[None, :], 0.0)
    weights = jnp.where(causal, jnp.exp(spread), 0.0)
    lower = jnp.where(strict, 2.0 * weights * exact_prod("ik,jk->ij", keys, keys), 0.0)
    system = lower + jnp.eye(size, dtype=jnp.float32)
    mixing = 2.0 * weights * exact_prod("ik,jk->ij", queries, keys)
    start_decay = jnp.exp(cumul)
    end_decay = jnp.exp(cumul[-1] - cumul)
    return (system, mixing, start_decay, end_decay, start_decay[-1])


def solve_lower(system, target):
    return lax.linalg.triangular_solve(
        system, target, left_side=True, lower=True, unit_diagonal=True
    )


def block_forward(queries, keys, values, start_state, gates):
    system, mixing, start_decay, end_decay, total = block_parts(queries, keys, gates)
    target = values - start_decay[:, None] * exact_prod("ik,kv->iv", keys, start_state)
    fresh = solve_lower(system, target)
    outputs = start_decay[:, None] * exact_prod("ik,kv->iv", queries, start_state) + exact_prod(
        "ij,jv->iv", mixing, fresh
    )
    end_state = total * start_state + 2.0 * exact_prod(
        "ik,iv->kv", keys, end_decay[:, None] * fresh
    )
    return (outputs, end_state)


def block_maps(queries, keys, values, gates, grad_out):
    system, mixing, start_decay, end_decay, total = block_parts(queries, keys, gates)
    width = keys.shape[1]
    both = solve_lower(system, jnp.concatenate([values, start_decay[:, None] * keys], axis=1))
    initial_amount = both[:, : values.shape[1]]
    weight = both[:, values.shape[1] :]
    transition = total * jnp.eye(width, dtype=jnp.float32) - 2.0 * exact_prod(
        "ik,ij->kj", keys, end_decay[:, None] * weight
    )
    displacement = 2.0 * exact_prod("ik,iv->kv", keys, end_decay[:, None] * initial_amount)
    inner = exact_prod("ij,iv->jv", mixing, grad_out)
    adjoint = exact_prod("ik,iv->kv", start_decay[:, None] * queries, grad_out) - exact_prod(
        "jk,jv->kv", weight, inner
    )
    return (transition, displacement, adjoint)


def block_grads(queries, keys, values, start_state, gates, grad_out, end_grad):

    def forward(query_part, key_part, value_part):
        return block_forward(query_part, key_part, value_part, start_state, gates)

    _, pullback = jax.vjp(forward, queries, keys, values)
    return pullback((grad_out, end_grad))


def batched(function):
    return jax.vmap(jax.vmap(function))


def compose(earlier, later):
    return (
        exact_prod("hij,hjk->hik", later[0], earlier[0]),
        exact_prod("hij,hjk->hik", later[0], earlier[1]) + later[1],
    )


def per_device(query_raw, key_raw, value_raw, query_gain, log_decay, out_grad):
    rows, width = query_raw.shape
    heads = log_decay.shape[0]
    head_dim = width // heads
    blocks = rows // BLOCK
    raw_query = query_raw.astype(jnp.float32)
    squares = taken_together(jnp.sum(raw_query * raw_query, axis=1), HEAD)
    inv_rms = lax.rsqrt(squares / D + epsilon)
    normed = raw_query * inv_rms[:, None]
    scale = head_dim ** (-0.5)
    queries = normed * query_gain * scale
    raw_key = key_raw.astype(jnp.float32).reshape(rows, heads, head_dim)
    key_scale = lax.rsqrt(jnp.sum(raw_key * raw_key, axis=2, keepdims=True) + epsilon)
    keys = raw_key * key_scale

    def to_blocks(array):
        return array.reshape(blocks, BLOCK, heads, head_dim).transpose(2, 0, 1, 3)

    query_blocks = to_blocks(queries)
    key_blocks = to_blocks(keys)
    value_blocks = to_blocks(value_raw.astype(jnp.float32))
    grad_blocks = to_blocks(out_grad.astype(jnp.float32))
    gate_blocks = log_decay.reshape(heads, blocks, BLOCK)
    transitions, displacements, adjoints = batched(block_maps)(
        query_blocks, key_blocks, value_blocks, gate_blocks, grad_blocks
    )
    trans_seq = jnp.moveaxis(transitions, 1, 0)
    offset_seq = jnp.moveaxis(displacements, 1, 0)
    adjoint_seq = jnp.moveaxis(adjoints, 1, 0)
    identity = jnp.broadcast_to(jnp.eye(head_dim, dtype=jnp.float32), (heads, head_dim, head_dim))
    zeros = jnp.zeros((heads, head_dim, head_dim), jnp.float32)

    def gather_step(carry, item):
        return (compose(carry, item), None)

    (device_map, device_offset), _ = lax.scan(
        gather_step, (identity, zeros), (trans_seq, offset_seq)
    )

    def collect_adjoint(carry, item):
        matrix, term = item
        return (exact_prod("hji,hjk->hik", matrix, carry) + term, None)

    device_adjoint, _ = lax.scan(collect_adjoint, zeros, (trans_seq, adjoint_seq), reverse=True)
    _, incoming = carried_in((device_map, device_offset), SEQ, compose, (identity, zeros))
    back_map = jnp.swapaxes(device_map, 1, 2)
    _, outgoing = carried_in_2((back_map, device_adjoint), SEQ, compose, (identity, zeros))

    def advance(state_matrix, item):
        matrix, shift = item
        return (exact_prod("hij,hjk->hik", matrix, state_matrix) + shift, state_matrix)

    def retreat(adjoint_state, item):
        matrix, term = item
        return (exact_prod("hji,hjk->hik", matrix, adjoint_state) + term, adjoint_state)

    _, starts = lax.scan(advance, incoming, (trans_seq, offset_seq))
    _, ends = lax.scan(retreat, outgoing, (trans_seq, adjoint_seq), reverse=True)
    query_grad, key_grad, value_grad = batched(block_grads)(
        query_blocks,
        key_blocks,
        value_blocks,
        jnp.moveaxis(starts, 0, 1),
        gate_blocks,
        grad_blocks,
        jnp.moveaxis(ends, 0, 1),
    )

    def from_blocks(array):
        return array.transpose(1, 2, 0, 3).reshape(rows, width)

    key_grad_rows = key_grad.transpose(1, 2, 0, 3).reshape(rows, heads, head_dim)
    key_raw_grad = key_scale * (
        key_grad_rows - keys * jnp.sum(keys * key_grad_rows, axis=2, keepdims=True)
    )
    key_raw_grad = key_raw_grad.reshape(rows, width).astype(jnp.bfloat16)
    value_raw_grad = from_blocks(value_grad).astype(jnp.bfloat16)
    scaled = from_blocks(query_grad) * query_gain * scale
    correction = by_axis(jnp.sum(scaled * normed, axis=1), HEAD) / D
    query_raw_grad = (inv_rms[:, None] * (scaled - normed * correction[:, None])).astype(
        jnp.bfloat16
    )
    return (
        lax.all_to_all(query_raw_grad, HEAD, split_axis=0, concat_axis=1, tiled=True),
        lax.all_to_all(key_raw_grad, HEAD, split_axis=0, concat_axis=1, tiled=True),
        lax.all_to_all(value_raw_grad, HEAD, split_axis=0, concat_axis=1, tiled=True),
    )


def solution(mesh):
    split = Mesh(mesh.devices.reshape(4, 2, 4, 4), ("seq_0", "seq_1", "head_0", "head_1"))
    return jax.shard_map(
        per_device,
        mesh=split,
        in_specs=(P(SEQ, HEAD), P(SEQ, HEAD), P(SEQ, HEAD), P(HEAD), P(HEAD, SEQ), P(SEQ, HEAD)),
        out_specs=(P(SEQ_HEAD, None), P(SEQ_HEAD, None), P(SEQ_HEAD, None)),
        check_vma=False,
    )
```

profile of v0, /device:TPU:0, one launch (start us, length us, event | category | flops | bytes accessed | tf_op | source)
XLA Modules:
  0.0 694.1 jit_solution(8259316048077969374)
XLA Ops:
  8.5 1.5 copy.281
  10.3 1.6 convert_bitcast_fusion
  15.5 1.6 copy.404
  18.5 1.8 copy.353
  20.4 1.9 copy.282
  22.3 2.2 bitcast_multiply_fusion.6
  24.6 6.5 add_bitcast_fusion.2
  31.1 315.8 %custom-call.8 = f32[4,8,1,128,128]{3,4,2,1,0:T(8,128)} custom-call(f32[4,8,1,128,128]{4,3,2,1,0:T(8,128)} %add_bitcast_fusion.2), custom_call_target="InvertDiagBlocksLowerTriangular" | custom-call | tf_op jit(solution)/shard_map/vmap(vmap())/triangular_solve | solution.py:91
  346.9 6.6 fusion.32
  353.5 5.4 multiply_bitcast_fusion.1
  359.0 4.7 bitcast_subtract_fusion
  363.7 1.8 copy.289
  365.7 1.5 copy.290
  367.2 22.9 %while.72 = (s32[]{:T(128)}, f32[4,128,128]{2,1,0:T(8,128)S(1)}, f32[4,128,128]{2,1,0:T(8,128)S(1)}, f32[8,4,128,128]{3,2,1,0:T(8,128)}, f32[8,4,128,128]{3,2,1,0:T(8,128)}, /*index=5*/s32[]{:T(128)}, s32[]{:T(128)}) while((s32[]{:T(128)}, f32[4,128,128]{2,1,0:T(8,128)S(1)}, f32[4,128,128]{2,1,0:T(8,128)S(1)}, ...), condition=%wide.region_5.6_spmd.clone, body=%wide.region_4.5_spmd.clone.sunk | while | flops 201457664 | bytes 2885218 | solution.py:181
  391.6 2.3 copy.277
  396.0 7.2 %all-to-all-start = ((f32[16,1,1024]{2,1,0:T(1,128)}), f32[16,1,1024]{2,1,0:T(1,128)}, u32[]{:S(2)}, u32[]{:S(2)}) async-start(f32[16,1,1024]{2,1,0:T(1,128)} %broadcast_in_dim.86), calls=%async_computation | async-start | bytes 131072 | tf_op jit(solution)/shard_map/all_to_all | solution.py:18
  403.4 2.2 all-gather.2
  408.3 3.0 copy.305
  412.7 1.6 reduce_sum.46
  415.5 3.4 all-gather.13.cloned.1.call-done
  419.0 27.4 %all-gather.11.cloned.1.call-done = f32[32,128,128]{2,1,0:T(8,128)} async-done(((f32[4,128,128]{2,1,0:T(8,128)}), f32[32,128,128]{2,1,0:T(8,128)}) %all-gather.11.cloned.1.call-update) | async-done | bytes 2097168 | tf_op jit(solution)/shard_map/all_gather | solution.py:29
  446.4 11.9 %while.73 = (s32[]{:T(128)}, f32[4,128,128]{2,1,0:T(8,128)S(1)}, s32[]{:T(128)}, f32[8,4,128,128]{3,2,1,0:T(8,128)}, f32[8,4,128,128]{3,2,1,0:T(8,128)}, /*index=5*/s32[]{:T(128)}, s32[]{:T(128)}) while((s32[]{:T(128)}, f32[4,128,128]{2,1,0:T(8,128)S(1)}, s32[]{:T(128)}, f32[8,4,128,128]{3,2,1,0:T(8,128)}, ...), condition=%wide.region_7.8_spmd.clone, body=%wide.region_6.7_spmd.clone.sunk | while | flops 100925440 | bytes 1837671 | solution.py:41
  458.3 1.6 broadcast.118.clone
  459.9 18.0 %while.70 = (s32[]{:T(128)}, f32[4,128,128]{2,1,0:T(8,128)S(1)}, f32[8,4,128,128]{3,2,1,0:T(8,128)}, f32[8,4,128,128]{3,2,1,0:T(8,128)}, f32[8,4,128,128]{3,2,1,0:T(8,128)}, /*index=5*/s32[]{:T(128)}) while((s32[]{:T(128)}, f32[4,128,128]{2,1,0:T(8,128)S(1)}, f32[8,4,128,128]{3,2,1,0:T(8,128)}, f32[8,4,128,128]{3,2,1,0:T(8,128)}, ...), condition=%wide.region_9.10_spmd, body=%wide.region_8.9_spmd.sunk | while | flops 100728832 | bytes 2098257 | solution.py:202
  477.9 4.0 fusion.72
  481.9 4.0 fusion.60
  486.0 2.4 bitcast_multiply_fusion.5
  488.5 2.2 fusion.70
  490.8 5.9 add_bitcast_fusion.1
  496.7 3.1 copy.297
  499.8 2.2 fusion.39
  502.0 10.4 %psum.14 = f32[1024]{0:T(1024)S(1)} all-reduce(f32[1024]{0:T(1024)S(1)} %fusion.39), channel_id=1, replica_groups=mesh['seq_0'=4,'seq_1'=2,'head_0'=4,'head_1'=4] {'head_0'}, use_global_device_ids=true, to_apply=%region_11.12 | all-reduce | flops 1024 | bytes 8192 | tf_op jit(solution)/shard_map/psum | solution.py:66
  512.4 10.5 %psum.15 = f32[1024]{0:T(1024)S(1)} all-reduce(f32[1024]{0:T(1024)S(1)} %psum.14), channel_id=1, replica_groups=mesh['seq_0'=4,'seq_1'=2,'head_0'=4,'head_1'=4] {'head_1'}, use_global_device_ids=true, to_apply=%region_12.13 | all-reduce | flops 1024 | bytes 8192 | tf_op jit(solution)/shard_map/psum | solution.py:66
  522.9 3.3 fusion.44
  526.2 1.8 copy.356
  528.0 3.0 copy.301
  531.0 6.2 fusion.53
  537.2 2.7 fusion.55
  540.0 2.5 fusion.82
  542.4 3.7 subtract_bitcast_fusion
  546.1 1.6 copy.306
  547.8 11.9 %while.74 = (s32[]{:T(128)}, f32[4,128,128]{2,1,0:T(8,128)S(1)}, f32[8,4,128,128]{2,3,1,0:T(8,128)}, f32[8,4,128,128]{3,2,1,0:T(8,128)}, s32[]{:T(128)}, /*index=5*/s32[]{:T(128)}, s32[]{:T(128)}) while((s32[]{:T(128)}, f32[4,128,128]{2,1,0:T(8,128)S(1)}, f32[8,4,128,128]{2,3,1,0:T(8,128)}, f32[8,4,128,128]{3,2,1,0:T(8,128)}, ...), condition=%wide.region_14.15_spmd.clone, body=%wide.region_13.14_spmd.clone.sunk | while | flops 100794368 | bytes 1574506 | solution.py:189
  547.8 1.5 convolution_add_fusion.19
  559.7 2.7 all-gather.4
  565.0 2.3 copy.298
  567.3 4.4 all-to-all-start.1
  571.6 7.1 %fusion.51 = f32[4,8,128,128]{3,2,1,0:T(8,128)} fusion(f32[4,8,128,128]{3,2,1,0:T(8,128)} %copy-done.27, f32[4,8,128,128]{2,1,3,0:T(8,128)} %bitcast.275), kind=kOutput, calls=%fused_computation.66 | convolution fusion | flops 805306368 | bytes 6291456 | tf_op jit(solution)/shard_map/vmap(vmap(transpose(jvp(ik,jk->ij))))/dot_general | solution.py:70
  578.8 5.5 all-gather.17.cloned.1.call-done
  589.0 1.5 broadcast.118
  590.5 17.6 %while.71 = (s32[]{:T(128)}, f32[4,128,128]{2,1,0:T(8,128)S(1)}, f32[8,4,128,128]{3,2,1,0:T(8,128)}, f32[8,4,128,128]{2,3,1,0:T(8,128)}, f32[8,4,128,128]{3,2,1,0:T(8,128)}, /*index=5*/s32[]{:T(128)}, s32[]{:T(128)}) while((s32[]{:T(128)}, f32[4,128,128]{2,1,0:T(8,128)S(1)}, f32[8,4,128,128]{3,2,1,0:T(8,128)}, ...), condition=%wide.region_16.17_spmd, body=%wide.region_15.16_spmd.sunk | while | flops 100728832 | bytes 2098269 | solution.py:203
  608.1 4.4 multiply_add_fusion
  612.5 2.2 fusion.58
  618.5 6.9 fusion.169
  625.4 5.8 fusion.84
  631.2 4.3 select_multiply_fusion
  635.5 7.0 %all-to-all-start.3 = ((bf16[16,64,512]{2,1,0:T(8,128)(2,1)}), bf16[16,64,512]{2,1,0:T(8,128)(2,1)S(1)}, u32[]{:S(2)}, u32[]{:S(2)}) async-start(bf16[16,64,512]{2,1,0:T(8,128)(2,1)} %convert_element_type.53), calls=%async_computation.3 | async-start | bytes 2097152 | tf_op jit(solution)/shard_map/all_to_all | solution.py:231
  642.5 6.7 fusion.79
  649.3 2.2 fusion.63
  651.5 6.1 multiply_reduce_fusion
  657.6 3.0 copy.321
  660.6 2.3 fusion.48
  664.2 7.3 %all-to-all-start.2 = ((bf16[16,64,512]{2,1,0:T(8,128)(2,1)}), bf16[16,64,512]{2,1,0:T(8,128)(2,1)S(1)}, u32[]{:S(2)}, u32[]{:S(2)}) async-start(bf16[16,64,512]{2,1,0:T(8,128)(2,1)} %bitcast.36), calls=%async_computation.2 | async-start | bytes 2097152 | tf_op jit(solution)/shard_map/all_to_all | solution.py:230
  671.6 2.3 copy.349
  674.9 11.3 %all-to-all-done.2 = bf16[16,64,512]{2,1,0:T(8,128)(2,1)S(1)} async-done(((bf16[16,64,512]{2,1,0:T(8,128)(2,1)}), bf16[16,64,512]{2,1,0:T(8,128)(2,1)S(1)}, u32[]{:S(2)}, u32[]{:S(2)}) %all-to-all-start.2) | async-done | bytes 1048608 | tf_op jit(solution)/shard_map/all_to_all | solution.py:230
  (274 shorter events, 109.3 us)
Async XLA Ops:
  7.2 411.8 %all-gather.13.cloned.1.call-start = ((), (), s32[]{:S(2)}) async-start(), calls=%async_computation.5 | async-start | bytes 2359296 | tf_op jit(solution)/shard_map/all_gather | solution.py:29
  10.0 1.9 copy-start.17
  10.0 1.9 copy-start.46
  10.0 4.7 copy-start.39
  15.4 4.9 copy-start.13
  15.4 3.1 copy-start.30
  22.3 2.3 copy-start.42
  22.3 2.3 copy-start.44
  22.3 2.3 copy-start.47
  22.3 2.2 copy-start.51
  353.5 5.5 copy-start.1
  353.5 5.5 copy-start.53
  363.7 2.0 copy-start.11
  390.1 0.7 copy-start.25
  390.1 0.8 copy-start.15
  390.8 55.6 %all-gather.11.cloned.1.call-start = ((), (), s32[]{:S(2)}) async-start(), calls=%async_computation.4 | async-start | bytes 2359296 | tf_op jit(solution)/shard_map/all_gather | solution.py:29
  391.6 11.7 %copy-start.16 = (f32[4,128,128]{2,1,0:T(8,128)S(1)}, f32[4,128,128]{2,1,0:T(8,128)}, u32[]{:S(2)}) copy-start(f32[4,128,128]{2,1,0:T(8,128)} %copy-done.15) | copy-start | bytes 786436
  396.0 16.7 %all-to-all-start = ((f32[16,1,1024]{2,1,0:T(1,128)}), f32[16,1,1024]{2,1,0:T(1,128)}, u32[]{:S(2)}, u32[]{:S(2)}) async-start(f32[16,1,1024]{2,1,0:T(1,128)} %broadcast_in_dim.86), calls=%async_computation | async-start | bytes 131072 | tf_op jit(solution)/shard_map/all_to_all | solution.py:18
  403.2 175.5 %all-gather.15.cloned.1.call-start = ((), (), s32[]{:S(2)}) async-start(), calls=%async_computation.6 | async-start | bytes 1310720 | tf_op jit(solution)/shard_map/all_gather | solution.py:55
  405.6 0.8 copy-start.20
  406.4 0.7 copy-start.37
  408.2 176.1 %all-gather.17.cloned.1.call-start = ((), (), s32[]{:S(2)}) async-start(), calls=%async_computation.7 | async-start | bytes 1310720 | tf_op jit(solution)/shard_map/all_gather | solution.py:55
  412.7 78.0 %copy-start.22 = (bf16[8,128,4,128]{3,2,1,0:T(4,128)(2,1)}, bf16[8,128,4,128]{3,2,1,0:T(4,128)(2,1)S(1)}, u32[]{:S(2)}) copy-start(bf16[8,128,4,128]{3,2,1,0:T(4,128)(2,1)S(1)} %reshape.159) | copy-start | bytes 3145732
  477.9 4.1 copy-start.4
  477.9 4.1 copy-start.14
  481.9 4.1 copy-start.48
  486.0 2.4 copy-start.7
  488.4 2.2 copy-start.27
  488.5 2.3 copy-start
  496.7 3.1 copy-start.19
  496.7 3.1 copy-start.43
  496.7 3.1 copy-start.54
  531.0 6.2 copy-start.10
  531.0 6.2 copy-start.23
  537.2 2.7 copy-start.49
  539.9 2.5 copy-start.2
  542.4 3.7 copy-start.31
  546.1 1.7 copy-start.24
  547.8 14.6 %copy-start.21 = (f32[8,128,128]{2,1,0:T(8,128)S(1)}, f32[8,128,128]{2,1,0:T(8,128)}, u32[]{:S(2)}) copy-start(f32[8,128,128]{2,1,0:T(8,128)} %copy-done.20) | copy-start | bytes 1572868
  559.6 4.3 copy-start.36
  559.7 4.3 copy-start.38
  562.7 4.5 copy-start.34
  567.3 68.2 %all-to-all-start.1 = ((bf16[16,64,512]{2,1,0:T(8,128)(2,1)}), bf16[16,64,512]{2,1,0:T(8,128)(2,1)}, u32[]{:S(2)}, u32[]{:S(2)}) async-start(bf16[16,64,512]{2,1,0:T(8,128)(2,1)} %bitcast.21), calls=%async_computation.1 | async-start | bytes 2097152 | tf_op jit(solution)/shard_map/all_to_all | solution.py:229
  578.8 8.4 %copy-start.32 = (f32[16,128,128]{2,1,0:T(8,128)S(1)}, f32[16,128,128]{2,1,0:T(8,128)}, u32[]{:S(2)}) copy-start(f32[16,128,128]{2,1,0:T(8,128)} %all-gather.15.cloned.1.call-done) | copy-start | bytes 3145732
  584.3 2.9 copy-start.40
  587.2 1.0 copy-start.41
  587.2 1.3 copy-start.33
  587.3 1.3 copy-start.35
  608.1 4.4 copy-start.5
  612.5 2.2 copy-start.9
  614.8 1.4 copy-start.3
  618.5 6.9 copy-start.8
  618.5 6.9 copy-start.12
  625.4 5.8 copy-start.6
  625.4 5.8 copy-start.45
  625.4 5.8 copy-start.50
  625.4 5.8 copy-start.52
  635.5 28.8 %all-to-all-start.3 = ((bf16[16,64,512]{2,1,0:T(8,128)(2,1)}), bf16[16,64,512]{2,1,0:T(8,128)(2,1)S(1)}, u32[]{:S(2)}, u32[]{:S(2)}) async-start(bf16[16,64,512]{2,1,0:T(8,128)(2,1)} %convert_element_type.53), calls=%async_computation.3 | async-start | bytes 2097152 | tf_op jit(solution)/shard_map/all_to_all | solution.py:231
  642.5 6.7 copy-start.29
  649.2 2.2 copy-start.26
  649.3 2.2 copy-start.28
  657.6 3.0 copy-start.18
  664.2 22.0 %all-to-all-start.2 = ((bf16[16,64,512]{2,1,0:T(8,128)(2,1)}), bf16[16,64,512]{2,1,0:T(8,128)(2,1)S(1)}, u32[]{:S(2)}, u32[]{:S(2)}) async-start(bf16[16,64,512]{2,1,0:T(8,128)(2,1)} %bitcast.36), calls=%async_computation.2 | async-start | bytes 2097152 | tf_op jit(solution)/shard_map/all_to_all | solution.py:230
Sparse Core Ops, SparseCore 0:
  390.9 27.9 all-gather.12
  420.7 25.6 all-gather.10
  448.1 24.5 all-gather.14
  564.0 20.2 all-gather.16
where the time goes:
time: 704 us; the launch traced here: 694 us
  other arithmetic  335 us (48%)
  matrix products  179 us (25%)
  local copies, waits for them, and re-layouts  62.9 us (9%)
  waiting for transfers between devices  48.4 us (7%)
  starting transfers between devices  26.1 us (4%)
  blocking collectives  25.8 us (4%)
  between operations  15 us (2%)
    another operation x4, other arithmetic, solve_lower(): lax.linalg.triangular_solve(system, target, left_side=True, lower=True, u...  317 us
    dot_general x76, matrix products, exact_prod(): return jnp.einsum(form, left, right, precision=lax.Precision.HIGHEST)  155 us
    all_gather x2, waiting for transfers between devices, carried_in(): everything = jax.tree.map(lambda part: lax.all_gather(part, axis), value)  30.9 us
    psum x2, blocking collectives, by_axis(): return functools.reduce(lax.psum, axes, value)  20.9 us
    unnamed x121, local copies, waits for them, and re-layouts  20.6 us
    another operation x4, matrix products, solve_lower(): lax.linalg.triangular_solve(system, target, left_side=True, lower=True, u...  17.1 us
  transfers between devices with their start and end apart: 8, of which 4 were waited for; matrix products, arithmetic and copies ran while one was open for 27% of the time, Pallas kernels for 0%

commit v1 on v0

--- a/solution.py
+++ b/solution.py
@@ -225,9 +225,18 @@
     query_raw_grad = (inv_rms[:, None] * (scaled - normed * correction[:, None])).astype(
         jnp.bfloat16
     )
+    words_number = lambda panel: jnp.concatenate(
+        lax.all_to_all(
+            jnp.stack(jnp.split(panel, lax.axis_size(HEAD), axis=0), 0),
+            split_axis=0,
+            concat_axis=0,
+            axis_name=HEAD,
+        ),
+        1,
+    )
     return (
         lax.all_to_all(query_raw_grad, HEAD, split_axis=0, concat_axis=1, tiled=True),
-        lax.all_to_all(key_raw_grad, HEAD, split_axis=0, concat_axis=1, tiled=True),
+        words_number(key_raw_grad),
         lax.all_to_all(value_raw_grad, HEAD, split_axis=0, concat_axis=1, tiled=True),
     )
 

time: 704 us -> 716 us (1.017)
  local copies, waits for them, and re-layouts: 62.9 us -> 74.7 us
  waiting for transfers between devices: 48.4 us -> 58.6 us
    unnamed x121 -> x128, local copies, waits for them, and re-layouts: 20.6 us -> 30.5 us
    all_to_all x1, waiting for transfers between devices: 0.01 us -> 8.84 us  [per_device(): lax.all_to_all(value_raw_grad, HEAD, split_axis=0, concat_axis=1, tiled=T...]
  transfers between devices with their start and end apart: 8 -> 8, of which waited for: 4 -> 5; matrix products, arithmetic and copies ran while one was open for 27% -> 28% of each run, Pallas kernels for 0% -> 0%
where the time goes in v1:
time: 716 us; the launch traced here: 705 us
  other arithmetic  335 us (47%)
  matrix products  172 us (24%)
  local copies, waits for them, and re-layouts  74.7 us (10%)
  waiting for transfers between devices  58.6 us (8%)
  blocking collectives  25.8 us (4%)
  starting transfers between devices  22.2 us (3%)
  between operations  14.9 us (2%)
    another operation x4, other arithmetic, solve_lower(): lax.linalg.triangular_solve(system, target, left_side=True, lower=True, u...  317 us
    dot_general x76, matrix products, exact_prod(): return jnp.einsum(form, left, right, precision=lax.Precision.HIGHEST)  151 us
    all_gather x2, waiting for transfers between devices, carried_in(): everything = jax.tree.map(lambda part: lax.all_gather(part, axis), value)  30.9 us
    unnamed x128, local copies, waits for them, and re-layouts  30.5 us
    psum x2, blocking collectives, by_axis(): return functools.reduce(lax.psum, axes, value)  20.9 us
    another operation x4, matrix products, solve_lower(): lax.linalg.triangular_solve(system, target, left_side=True, lower=True, u...  16 us
  transfers between devices with their start and end apart: 8, of which 5 were waited for; matrix products, arithmetic and copies ran while one was open for 28% of the time, Pallas kernels for 0%

profile of v1, /device:TPU:0, one launch (start us, length us, event | category | flops | bytes accessed | tf_op | source)
XLA Modules:
  0.0 705.2 jit_solution(7479147862705647702)
XLA Ops:
  10.3 1.6 convert_bitcast_fusion
  15.4 1.7 copy.450
  18.5 1.8 copy.399
  20.3 1.9 copy.328
  22.3 2.2 bitcast_multiply_fusion.6
  24.5 6.5 add_bitcast_fusion.2
  31.0 315.8 %custom-call.8 = f32[4,8,1,128,128]{3,4,2,1,0:T(8,128)} custom-call(f32[4,8,1,128,128]{4,3,2,1,0:T(8,128)} %add_bitcast_fusion.2), custom_call_target="InvertDiagBlocksLowerTriangular" | custom-call | tf_op jit(solution)/shard_map/vmap(vmap())/triangular_solve | solution.py:91
  346.9 6.6 fusion.32
  353.5 5.4 multiply_bitcast_fusion.1
  358.9 4.7 bitcast_subtract_fusion
  363.7 1.8 copy.335
  365.6 1.5 copy.336
  367.2 22.9 %while.72 = (s32[]{:T(128)}, f32[4,128,128]{2,1,0:T(8,128)S(1)}, f32[4,128,128]{2,1,0:T(8,128)S(1)}, f32[8,4,128,128]{3,2,1,0:T(8,128)}, f32[8,4,128,128]{3,2,1,0:T(8,128)}, /*index=5*/s32[]{:T(128)}, s32[]{:T(128)}) while((s32[]{:T(128)}, f32[4,128,128]{2,1,0:T(8,128)S(1)}, f32[4,128,128]{2,1,0:T(8,128)S(1)}, ...), condition=%wide.region_5.6_spmd.clone, body=%wide.region_4.5_spmd.clone.sunk | while | flops 201457664 | bytes 2885218 | solution.py:181
  391.5 2.3 copy.323
  396.0 7.2 %all-to-all-start = ((f32[16,1,1024]{2,1,0:T(1,128)}), f32[16,1,1024]{2,1,0:T(1,128)}, u32[]{:S(2)}, u32[]{:S(2)}) async-start(f32[16,1,1024]{2,1,0:T(1,128)} %broadcast_in_dim.86), calls=%async_computation | async-start | bytes 131072 | tf_op jit(solution)/shard_map/all_to_all | solution.py:18
  403.4 2.2 all-gather.2
  408.3 3.0 copy.351
  412.7 1.6 reduce_sum.46
  415.5 3.4 all-gather.13.cloned.1.call-done
  419.0 27.5 %all-gather.11.cloned.1.call-done = f32[32,128,128]{2,1,0:T(8,128)} async-done(((f32[4,128,128]{2,1,0:T(8,128)}), f32[32,128,128]{2,1,0:T(8,128)}) %all-gather.11.cloned.1.call-update) | async-done | bytes 2097168 | tf_op jit(solution)/shard_map/all_gather | solution.py:29
  446.5 11.9 %while.73 = (s32[]{:T(128)}, f32[4,128,128]{2,1,0:T(8,128)S(1)}, s32[]{:T(128)}, f32[8,4,128,128]{3,2,1,0:T(8,128)}, f32[8,4,128,128]{3,2,1,0:T(8,128)}, /*index=5*/s32[]{:T(128)}, s32[]{:T(128)}) while((s32[]{:T(128)}, f32[4,128,128]{2,1,0:T(8,128)S(1)}, s32[]{:T(128)}, f32[8,4,128,128]{3,2,1,0:T(8,128)}, ...), condition=%wide.region_7.8_spmd.clone, body=%wide.region_6.7_spmd.clone.sunk | while | flops 100925440 | bytes 1837671 | solution.py:41
  458.3 1.6 broadcast.118.clone
  459.9 18.0 %while.70 = (s32[]{:T(128)}, f32[4,128,128]{2,1,0:T(8,128)S(1)}, f32[8,4,128,128]{3,2,1,0:T(8,128)}, f32[8,4,128,128]{3,2,1,0:T(8,128)}, f32[8,4,128,128]{3,2,1,0:T(8,128)}, /*index=5*/s32[]{:T(128)}) while((s32[]{:T(128)}, f32[4,128,128]{2,1,0:T(8,128)S(1)}, f32[8,4,128,128]{3,2,1,0:T(8,128)}, f32[8,4,128,128]{3,2,1,0:T(8,128)}, ...), condition=%wide.region_9.10_spmd, body=%wide.region_8.9_spmd.sunk | while | flops 100728832 | bytes 2098257 | solution.py:202
  477.9 4.0 fusion.72
  482.0 4.0 fusion.60
  486.0 2.4 bitcast_multiply_fusion.5
  488.5 2.2 fusion.70
  490.8 5.9 add_bitcast_fusion.1
  496.7 3.1 copy.343
  499.8 2.2 fusion.39
  501.9 10.4 %psum.14 = f32[1024]{0:T(1024)S(1)} all-reduce(f32[1024]{0:T(1024)S(1)} %fusion.39), channel_id=1, replica_groups=mesh['seq_0'=4,'seq_1'=2,'head_0'=4,'head_1'=4] {'head_0'}, use_global_device_ids=true, to_apply=%region_11.12 | all-reduce | flops 1024 | bytes 8192 | tf_op jit(solution)/shard_map/psum | solution.py:66
  512.4 10.5 %psum.15 = f32[1024]{0:T(1024)S(1)} all-reduce(f32[1024]{0:T(1024)S(1)} %psum.14), channel_id=1, replica_groups=mesh['seq_0'=4,'seq_1'=2,'head_0'=4,'head_1'=4] {'head_1'}, use_global_device_ids=true, to_apply=%region_12.13 | all-reduce | flops 1024 | bytes 8192 | tf_op jit(solution)/shard_map/psum | solution.py:66
  522.8 3.3 fusion.44
  526.2 1.8 copy.402
  528.0 3.0 copy.347
  530.9 6.2 fusion.53
  537.2 2.7 fusion.55
  539.9 2.5 fusion.82
  542.4 3.7 subtract_bitcast_fusion
  546.1 1.6 copy.352
  547.6 11.9 %while.74 = (s32[]{:T(128)}, f32[4,128,128]{2,1,0:T(8,128)S(1)}, f32[8,4,128,128]{2,3,1,0:T(8,128)}, f32[8,4,128,128]{3,2,1,0:T(8,128)}, s32[]{:T(128)}, /*index=5*/s32[]{:T(128)}, s32[]{:T(128)}) while((s32[]{:T(128)}, f32[4,128,128]{2,1,0:T(8,128)S(1)}, f32[8,4,128,128]{2,3,1,0:T(8,128)}, f32[8,4,128,128]{3,2,1,0:T(8,128)}, ...), condition=%wide.region_14.15_spmd.clone, body=%wide.region_13.14_spmd.clone.sunk | while | flops 100794368 | bytes 1574506 | solution.py:189
  559.5 2.7 all-gather.4
  564.8 2.3 copy.344
  567.1 4.3 all-to-all-start.1
  571.5 7.2 %fusion.51 = f32[4,8,128,128]{3,2,1,0:T(8,128)} fusion(f32[4,8,128,128]{3,2,1,0:T(8,128)} %copy-done.24, f32[4,8,128,128]{2,1,3,0:T(8,128)} %bitcast.338), kind=kOutput, calls=%fused_computation.66 | convolution fusion | flops 805306368 | bytes 6291456 | tf_op jit(solution)/shard_map/vmap(vmap(transpose(jvp(ik,jk->ij))))/dot_general | solution.py:70
  578.7 5.5 all-gather.17.cloned.1.call-done
  588.9 1.6 broadcast.118
  590.4 17.6 %while.71 = (s32[]{:T(128)}, f32[4,128,128]{2,1,0:T(8,128)S(1)}, f32[8,4,128,128]{3,2,1,0:T(8,128)}, f32[8,4,128,128]{2,3,1,0:T(8,128)}, f32[8,4,128,128]{3,2,1,0:T(8,128)}, /*index=5*/s32[]{:T(128)}, s32[]{:T(128)}) while((s32[]{:T(128)}, f32[4,128,128]{2,1,0:T(8,128)S(1)}, f32[8,4,128,128]{3,2,1,0:T(8,128)}, ...), condition=%wide.region_16.17_spmd, body=%wide.region_15.16_spmd.sunk | while | flops 100728832 | bytes 2098269 | solution.py:203
  608.1 4.6 multiply_add_fusion
  612.7 4.4 fusion.84
  617.1 4.5 fusion.185
  621.6 2.3 fusion.58
  623.9 4.4 fusion.79
  629.1 3.1 select_multiply_fusion
  632.2 2.2 fusion.63
  634.4 6.1 multiply_reduce_fusion
  640.5 3.0 copy.367
  643.5 2.3 fusion.48
  655.8 6.8 all-to-all-start.3
  666.3 2.7 copy.368
  668.9 8.8 %all-to-all-done.3 = bf16[16,64,512]{2,1,0:T(8,128)(2,1)S(1)} async-done(((bf16[16,64,512]{2,1,0:T(8,128)(2,1)}), bf16[16,64,512]{2,1,0:T(8,128)(2,1)S(1)}, u32[]{:S(2)}, u32[]{:S(2)}) %all-to-all-start.3) | async-done | bytes 1048608 | tf_op jit(solution)/shard_map/all_to_all | solution.py:240
  677.8 3.7 all-to-all-start.2
  681.4 2.3 copy.395
  684.8 12.6 %all-to-all-done.2 = bf16[16,64,512]{2,1,0:T(8,128)(2,1)S(1)} async-done(((bf16[16,64,512]{2,1,0:T(8,128)(2,1)}), bf16[16,64,512]{2,1,0:T(8,128)(2,1)S(1)}, u32[]{:S(2)}, u32[]{:S(2)}) %all-to-all-start.2) | async-done | bytes 1048608 | tf_op jit(solution)/shard_map/all_to_all | solution.py:229
  (282 shorter events, 121.5 us)
Async XLA Ops:
  7.2 411.8 %all-gather.13.cloned.1.call-start = ((), (), s32[]{:S(2)}) async-start(), calls=%async_computation.5 | async-start | bytes 2359296 | tf_op jit(solution)/shard_map/all_gather | solution.py:29
  10.0 1.9 copy-start.15
  10.0 1.9 copy-start.42
  10.0 4.7 copy-start.35
  15.4 4.9 copy-start.11
  15.4 3.1 copy-start.26
  22.3 2.3 copy-start.38
  22.3 2.3 copy-start.40
  22.3 2.3 copy-start.43
  22.3 2.3 copy-start.47
  353.5 5.5 copy-start.2
  353.5 5.5 copy-start.49
  363.7 2.0 copy-start.9
  390.1 0.7 copy-start.23
  390.1 0.8 copy-start.13
  390.8 55.7 %all-gather.11.cloned.1.call-start = ((), (), s32[]{:S(2)}) async-start(), calls=%async_computation.4 | async-start | bytes 2359296 | tf_op jit(solution)/shard_map/all_gather | solution.py:29
  391.5 11.7 %copy-start.14 = (f32[4,128,128]{2,1,0:T(8,128)S(1)}, f32[4,128,128]{2,1,0:T(8,128)}, u32[]{:S(2)}) copy-start(f32[4,128,128]{2,1,0:T(8,128)} %copy-done.13) | copy-start | bytes 786436
  396.0 16.7 %all-to-all-start = ((f32[16,1,1024]{2,1,0:T(1,128)}), f32[16,1,1024]{2,1,0:T(1,128)}, u32[]{:S(2)}, u32[]{:S(2)}) async-start(f32[16,1,1024]{2,1,0:T(1,128)} %broadcast_in_dim.86), calls=%async_computation | async-start | bytes 131072 | tf_op jit(solution)/shard_map/all_to_all | solution.py:18
  403.2 175.5 %all-gather.15.cloned.1.call-start = ((), (), s32[]{:S(2)}) async-start(), calls=%async_computation.6 | async-start | bytes 1310720 | tf_op jit(solution)/shard_map/all_gather | solution.py:55
  405.6 0.8 copy-start.18
  406.4 0.7 copy-start.33
  408.2 175.9 %all-gather.17.cloned.1.call-start = ((), (), s32[]{:S(2)}) async-start(), calls=%async_computation.7 | async-start | bytes 1310720 | tf_op jit(solution)/shard_map/all_gather | solution.py:55
  412.7 78.0 %copy-start.20 = (bf16[8,128,4,128]{3,2,1,0:T(4,128)(2,1)}, bf16[8,128,4,128]{3,2,1,0:T(4,128)(2,1)S(1)}, u32[]{:S(2)}) copy-start(bf16[8,128,4,128]{3,2,1,0:T(4,128)(2,1)S(1)} %reshape.164) | copy-start | bytes 3145732
  477.9 4.1 copy-start.4
  477.9 4.1 copy-start.12
  482.0 4.1 copy-start.44
  486.0 2.4 copy-start.6
  488.5 2.2 copy-start.24
  488.5 2.3 copy-start
  496.7 3.1 copy-start.17
  496.7 3.1 copy-start.39
  496.7 3.1 copy-start.50
  530.9 6.2 copy-start.8
  530.9 6.2 copy-start.21
  537.2 2.7 copy-start.45
  539.9 2.5 copy-start.3
  542.4 3.7 copy-start.27
  546.1 1.6 copy-start.22
  547.6 14.6 %copy-start.19 = (f32[8,128,128]{2,1,0:T(8,128)S(1)}, f32[8,128,128]{2,1,0:T(8,128)}, u32[]{:S(2)}) copy-start(f32[8,128,128]{2,1,0:T(8,128)} %copy-done.18) | copy-start | bytes 1572868
  559.5 4.2 copy-start.32
  559.5 4.2 copy-start.34
  562.6 4.5 copy-start.30
  567.1 88.7 %all-to-all-start.1 = ((bf16[16,64,512]{2,1,0:T(8,128)(2,1)}), bf16[16,64,512]{2,1,0:T(8,128)(2,1)}, u32[]{:S(2)}, u32[]{:S(2)}) async-start(bf16[16,64,512]{2,1,0:T(8,128)(2,1)} %bitcast.21), calls=%async_computation.1 | async-start | bytes 2097152 | tf_op jit(solution)/shard_map/all_to_all | solution.py:238
  578.7 8.4 %copy-start.28 = (f32[16,128,128]{2,1,0:T(8,128)S(1)}, f32[16,128,128]{2,1,0:T(8,128)}, u32[]{:S(2)}) copy-start(f32[16,128,128]{2,1,0:T(8,128)} %all-gather.15.cloned.1.call-done) | copy-start | bytes 3145732
  584.2 2.9 copy-start.36
  587.1 1.0 copy-start.37
  587.1 1.3 copy-start.29
  587.1 1.3 copy-start.31
  608.0 4.6 copy-start.7
  608.1 4.6 copy-start.10
  617.1 4.5 copy-start.5
  621.6 2.3 copy-start.1
  628.3 0.7 copy-start.41
  628.3 0.7 copy-start.46
  628.3 0.7 copy-start.48
  632.2 2.2 copy-start.25
  640.5 3.0 copy-start.16
  655.8 22.0 %all-to-all-start.3 = ((bf16[16,64,512]{2,1,0:T(8,128)(2,1)}), bf16[16,64,512]{2,1,0:T(8,128)(2,1)S(1)}, u32[]{:S(2)}, u32[]{:S(2)}) async-start(bf16[16,64,512]{2,1,0:T(8,128)(2,1)} %convert_element_type.53), calls=%async_computation.3 | async-start | bytes 2097152 | tf_op jit(solution)/shard_map/all_to_all | solution.py:240
  677.8 19.6 %all-to-all-start.2 = ((bf16[16,64,512]{2,1,0:T(8,128)(2,1)}), bf16[16,64,512]{2,1,0:T(8,128)(2,1)S(1)}, u32[]{:S(2)}, u32[]{:S(2)}) async-start(bf16[16,64,512]{2,1,0:T(8,128)(2,1)} %copy.368), calls=%async_computation.2 | async-start | bytes 2097152 | tf_op jit(solution)/shard_map/all_to_all | solution.py:229
Sparse Core Ops, SparseCore 0:
  390.9 28.0 all-gather.12
  420.7 25.7 all-gather.10
  448.1 24.5 all-gather.14
  563.9 20.2 all-gather.16
